TPU v7x, 256 devices: a whole 4x4x8 slice. The times are simulated.
256 devices in a mesh: ent: 64 (over z, y, core), rel: 4 (over x).
Axes of the slice: x: 4, y: 4, z: 8, core: 2. Of those that a mesh axis runs over, the one named last changes fastest.
Arguments:
- entity_rows: bfloat16 [65536, 256], P('ent'), may hold values from -2.5 to 2.5
- request_rows: int32 [64, 64, 32], P('ent'), may hold values from 0 to 1023
- edge_heads: int32 [262144], P(('ent', 'rel')), may hold values from 0 to 1023
- edge_rels: int32 [262144], P(('ent', 'rel')), may hold values from 0 to 7
- edge_tails: int32 [262144], P(('ent', 'rel')), may hold values from 0 to 2047
- edge_counts: int32 [256], P(('ent', 'rel')), may hold values from 1 to 1024, 163840 in all
- negative_rows: int32 [65536], P(('ent', 'rel')), may hold values from 0 to 1023
- relation_blocks: bfloat16 [32, 8, 32, 32], P('rel'), may hold values from -1 to 1
Outputs:
- entity_grad: float32 [65536, 256], P('ent')
- relation_grad: float32 [32, 8, 32, 32], P('rel')
Inputs may be any that keep to these rules, and one draw needn't show every extreme that they name: Edge slots of bucket b at or past edge_counts[b] are ignored; some bucket is full in every draw.
All inputs are finite; a program needn't handle non-finite values. No bound on the sum of `edge_counts` on one device may be relied on, other than what follows from the above.
Results may differ from a plain program's by a relative error of at most 0.009.
Values may be sent and summed in bfloat16 or wider, within the bound.
No kernel may reach another device: no remote copies, remote signals or barrier semaphores. Data moves between devices by JAX's collectives and lax.ppermute only.
A program may use at most 64 MiB of HBM per device.

v0:
```python
import math
import jax
import jax.numpy as jnp
from jax import lax
from jax.sharding import PartitionSpec as P


def pick_rows(indices, source_table):
    row_total = indices.shape[0]
    block_size = math.gcd(row_total, 256)
    grouped = indices.reshape(row_total // block_size, block_size)
    columns = jnp.arange(source_table.shape[0], dtype=jnp.int32)

    def pick_block(index_block):
        one_hot = (index_block[:, None] == columns[None, :]).astype(jnp.bfloat16)
        return jnp.dot(one_hot, source_table, preferred_element_type=jnp.float32).astype(
            jnp.bfloat16
        )

    picked = lax.map(pick_block, grouped)
    return picked.reshape(row_total, source_table.shape[1])


def owner_add(indices, gradients, entity_count):
    start_value = jnp.zeros((entity_count, gradients.shape[1]), jnp.float32)
    return start_value.at[indices].add(gradients)


def local(
    entity_rows,
    request_rows,
    edge_heads,
    edge_rels,
    edge_tails,
    edge_counts,
    negative_rows,
    relation_blocks,
):
    entity_count, feature_width = entity_rows.shape
    part_count = request_rows.shape[1]
    slot_count = request_rows.shape[2]
    r_count, block_count, block_width = (
        relation_blocks.shape[0],
        relation_blocks.shape[1],
        relation_blocks.shape[2],
    )
    neg_count = negative_rows.shape[0]
    owner_lists = lax.all_to_all(request_rows, "ent", split_axis=1, concat_axis=0, tiled=True)
    wanted = pick_rows(owner_lists.reshape(-1), entity_rows).reshape(
        part_count, 1, slot_count, feature_width
    )
    fetched = lax.all_to_all(wanted, "ent", split_axis=0, concat_axis=1, tiled=True)
    fetched = fetched.reshape(part_count * slot_count, feature_width)
    neg_rows = pick_rows(negative_rows, entity_rows)
    edge_dev = edge_heads.shape[0]
    block_size = math.gcd(edge_dev, 256)
    block_total = edge_dev // block_size
    live_count = edge_counts[0]
    positions = jnp.arange(edge_dev, dtype=jnp.int32).reshape(block_total, block_size)
    entity_columns = jnp.arange(entity_count, dtype=jnp.int32)
    slot_columns = jnp.arange(part_count * slot_count, dtype=jnp.int32)
    rel_columns = jnp.arange(r_count, dtype=jnp.int32)
    contract_rows = (((0,), (0,)), ((), ()))

    def edge_block(running, block_inputs):
        slot_acc, entity_acc, neg_acc, relation_acc = running
        head_ids, rel_ids, tail_ids, places = block_inputs
        live_mask = (places < live_count).astype(jnp.float32)
        head_hot = (head_ids[:, None] == entity_columns[None, :]).astype(jnp.bfloat16)
        tail_hot = (tail_ids[:, None] == slot_columns[None, :]).astype(jnp.bfloat16)
        head_rows = jnp.dot(head_hot, entity_rows, preferred_element_type=jnp.float32).astype(
            jnp.bfloat16
        )
        tail_rows = jnp.dot(tail_hot, fetched, preferred_element_type=jnp.float32).astype(
            jnp.bfloat16
        )
        rel_hot = (rel_ids[:, None] == rel_columns[None, :]).astype(jnp.float32)
        head_split = head_rows.reshape(block_size, block_count, block_width)
        proj_all = jnp.einsum(
            "enb,rnbc->renc", head_split, relation_blocks, preferred_element_type=jnp.float32
        )
        projected = (
            jnp.sum(rel_hot.T[:, :, None, None] * proj_all, 0)
            .reshape(block_size, feature_width)
            .astype(jnp.bfloat16)
        )
        projected_wide = projected.astype(jnp.float32)
        positive = jnp.sum(projected_wide * tail_rows.astype(jnp.float32), -1)
        negative = lax.dot_general(
            projected, neg_rows, (((1,), (1,)), ((), ())), preferred_element_type=jnp.float32
        )
        pos_weight = -live_mask * jax.nn.sigmoid(-positive)
        neg_weight = (live_mask[:, None] * jax.nn.sigmoid(negative) / neg_count).astype(
            jnp.bfloat16
        )
        grad_proj = (
            pos_weight[:, None] * tail_rows.astype(jnp.float32)
            + jnp.dot(neg_weight, neg_rows, preferred_element_type=jnp.float32)
        ).astype(jnp.bfloat16)
        weighted = (pos_weight[:, None] * projected_wide).astype(jnp.bfloat16)
        grad_split = grad_proj.reshape(block_size, block_count, block_width)
        back_all = jnp.einsum(
            "enc,rnbc->renb", grad_split, relation_blocks, preferred_element_type=jnp.float32
        )
        head_grad = (
            jnp.sum(rel_hot.T[:, :, None, None] * back_all, 0)
            .reshape(block_size, feature_width)
            .astype(jnp.bfloat16)
        )
        slot_acc = slot_acc + lax.dot_general(
            tail_hot, weighted, contract_rows, preferred_element_type=jnp.float32
        )
        entity_acc = entity_acc + lax.dot_general(
            head_hot, head_grad, contract_rows, preferred_element_type=jnp.float32
        )
        neg_acc = neg_acc + lax.dot_general(
            neg_weight, projected, contract_rows, preferred_element_type=jnp.float32
        )
        masked_heads = rel_hot.T.astype(jnp.bfloat16)[:, :, None, None] * head_split[None]
        relation_acc = relation_acc + jnp.einsum(
            "renb,enc->rnbc", masked_heads, grad_split, preferred_element_type=jnp.float32
        )
        return ((slot_acc, entity_acc, neg_acc, relation_acc), None)

    start_values = (
        jnp.zeros((part_count * slot_count, feature_width), jnp.float32),
        jnp.zeros((entity_count, feature_width), jnp.float32),
        jnp.zeros((neg_count, feature_width), jnp.float32),
        jnp.zeros(relation_blocks.shape, jnp.float32),
    )
    block_inputs = (
        edge_heads.reshape(block_total, block_size),
        edge_rels.reshape(block_total, block_size),
        edge_tails.reshape(block_total, block_size),
        positions,
    )
    (slot_acc, entity_acc, neg_acc, relation_acc), _ = lax.scan(
        edge_block, start_values, block_inputs
    )
    neg_hot = (negative_rows[:, None] == entity_columns[None, :]).astype(jnp.bfloat16)
    entity_acc = entity_acc + lax.dot_general(
        neg_hot, neg_acc.astype(jnp.bfloat16), contract_rows, preferred_element_type=jnp.float32
    )
    slot_grads = slot_acc.reshape(1, part_count, slot_count, feature_width)
    returned = lax.all_to_all(
        slot_grads.astype(jnp.bfloat16), "ent", split_axis=1, concat_axis=0, tiled=True
    ).astype(slot_grads.dtype)
    entity_acc = entity_acc + owner_add(
        owner_lists.reshape(-1), returned.reshape(-1, feature_width), entity_count
    )
    entity_grad = lax.psum(entity_acc, "rel")
    relation_grad = lax.psum(relation_acc, "ent")
    return (entity_grad, relation_grad)


def solution(mesh):
    in_specs = (
        P("ent", None),
        P("ent", None, None),
        P(("ent", "rel")),
        P(("ent", "rel")),
        P(("ent", "rel")),
        P(("ent", "rel")),
        P(("ent", "rel")),
        P("rel", None, None, None),
    )
    out_specs = (P("ent", None), P("rel", None, None, None))
    return jax.shard_map(local, mesh=mesh, in_specs=in_specs, out_specs=out_specs, check_vma=False)
```

profile of v0, /device:TPU:8, one launch (start us, length us, event | category | flops | bytes accessed | tf_op | source)
XLA Modules:
  0.0 383.0 jit_solution(16212449031649504692)
XLA Ops:
  7.2 1.4 copy.20
  8.6 12.1 %all-to-all-start = ((s32[1,64,32]{2,0,1:T(1,128)}), s32[1,64,32]{2,0,1:T(1,128)S(1)}, u32[]{:S(2)}, u32[]{:S(2)}) async-start(s32[1,64,32]{2,0,1:T(1,128)} %copy.20), calls=%async_computation | async-start | bytes 65536 | tf_op jit(solution)/shard_map/all_to_all | solution.py:48
  20.7 8.5 %all-to-all-done = s32[1,64,32]{2,0,1:T(1,128)S(1)} async-done(((s32[1,64,32]{2,0,1:T(1,128)}), s32[1,64,32]{2,0,1:T(1,128)S(1)}, u32[]{:S(2)}, u32[]{:S(2)}) %all-to-all-start) | async-done | bytes 8224 | tf_op jit(solution)/shard_map/all_to_all | solution.py:48
  29.2 0.5 broadcast.122
  29.8 0.7 reduce.5
  30.6 16.5 %while.32 = (s32[]{:T(128)}, bf16[8,256,256]{2,1,0:T(8,128)(2,1)}, s32[8,256]{1,0:T(8,128)S(1)}, bf16[1024,256]{1,0:T(8,128)(2,1)}, s32[]{:T(128)}) while((s32[]{:T(128)}, bf16[8,256,256]{2,1,0:T(8,128)(2,1)}, s32[8,256]{1,0:T(8,128)S(1)}, bf16[1024,256]{1,0:T(8,128)(2,1)}, s32[]{:T(128)}) %tuple.56), condition=%wide.region_1.2_spmd.clone, body=%wide.region_0.1_spmd.clone.sunk | while | flops 134545408 | bytes 658509 | solution.py:20
  30.6 2.1 fusion.90
  32.6 2.0 fusion.90
  34.7 2.0 fusion.90
  36.8 2.1 fusion.90
  38.8 2.1 fusion.90
  40.9 2.0 fusion.90
  42.9 2.0 fusion.90
  45.0 2.1 fusion.90
  47.0 6.5 %all-to-all-start.1 = ((bf16[64,1,32,256]{3,2,1,0:T(8,128)(2,1)}), bf16[64,1,32,256]{3,2,1,0:T(8,128)(2,1)}, u32[]{:S(2)}, u32[]{:S(2)}) async-start(bf16[64,1,32,256]{3,2,1,0:T(8,128)(2,1)} %bitcast.1), calls=%async_computation.1 | async-start | bytes 2097152 | tf_op jit(solution)/shard_map/all_to_all | solution.py:52
  53.6 1.9 copy.21
  55.5 1.4 convolution_convert_fusion.2
  56.9 25.4 %all-to-all-done.1 = bf16[64,1,32,256]{3,2,1,0:T(8,128)(2,1)} async-done(((bf16[64,1,32,256]{3,2,1,0:T(8,128)(2,1)}), bf16[64,1,32,256]{3,2,1,0:T(8,128)(2,1)}, u32[]{:S(2)}, u32[]{:S(2)}) %all-to-all-start.1) | async-done | bytes 1048608 | tf_op jit(solution)/shard_map/all_to_all | solution.py:52
  82.3 38.9 %while.33 = (s32[]{:T(128)}, f32[2048,256]{1,0:T(8,128)S(1)}, f32[1024,256]{1,0:T(8,128)S(1)}, f32[256,256]{1,0:T(8,128)S(1)}, f32[8,8,32,32]{2,3,0,1:T(8,128)},...) while((s32[]{:T(128)}, f32[2048,256]{1,0:T(8,128)S(1)}, ...), condition=%wide.region_6.7_spmd.clone, body=%wide.region_2.6_spmd.clone.sunk | while | flops 1016077568 | bytes 14733582 | solution.py:137
  82.3 0.7 compare_convert_fusion.2
  83.0 1.5 convolution_convert_fusion.4
  84.5 1.5 fusion.110
  86.1 0.3 fusion.112
  86.6 2.1 fusion.111
  89.0 0.4 fusion.114
  89.4 0.9 fusion.115
  90.4 0.6 convolution_add_fusion.9
  90.9 1.1 convolution_add_fusion.8
  92.0 0.7 compare_convert_fusion.2
  92.8 1.5 convolution_convert_fusion.4
  94.3 1.5 fusion.110
  95.8 0.3 fusion.112
  96.4 2.1 fusion.111
  98.7 0.4 fusion.114
  99.1 0.9 fusion.115
  100.1 0.6 convolution_add_fusion.9
  100.7 1.1 convolution_add_fusion.8
  101.8 0.7 compare_convert_fusion.2
  102.5 1.5 convolution_convert_fusion.4
  104.0 1.5 fusion.110
  106.1 2.1 fusion.111
  108.4 0.4 fusion.114
  108.9 0.9 fusion.115
  109.8 0.6 convolution_add_fusion.9
  110.4 1.1 convolution_add_fusion.8
  111.5 0.7 compare_convert_fusion.2
  112.2 1.5 convolution_convert_fusion.4
  113.7 1.5 fusion.110
  115.8 2.1 fusion.111
  118.2 0.4 fusion.114
  118.6 0.9 fusion.115
  119.6 0.6 convolution_add_fusion.9
  120.2 1.1 convolution_add_fusion.8
  121.2 1.1 convert_element_type.106
  122.3 5.9 %all-to-all-start.2 = ((bf16[1,64,32,256]{3,2,0,1:T(8,128)(2,1)}), bf16[1,64,32,256]{3,2,0,1:T(8,128)(2,1)S(1)}, u32[]{:S(2)}, u32[]{:S(2)}) async-start(bf16[1,64,32,256]{3,2,0,1:T(8,128)(2,1)} %bitcast.124), calls=%async_computation.2 | async-start | bytes 2097152 | tf_op jit(solution)/shard_map/all_to_all | solution.py:145
  128.4 1.4 copy.22
  129.8 0.6 convolution_add_fusion.4
  130.4 27.4 %all-to-all-done.2 = bf16[1,64,32,256]{3,2,0,1:T(8,128)(2,1)S(1)} async-done(((bf16[1,64,32,256]{3,2,0,1:T(8,128)(2,1)}), bf16[1,64,32,256]{3,2,0,1:T(8,128)(2,1)S(1)}, u32[]{:S(2)}, u32[]{:S(2)}) %all-to-all-start.2) | async-done | bytes 1048608 | tf_op jit(solution)/shard_map/all_to_all | solution.py:145
  157.7 12.0 %scatter_custom_fusion = f32[1024,256]{1,0:T(8,128)S(1)} fusion(f32[1024,256]{1,0:T(8,128)S(1)} %convolution_add_fusion.4, s32[2048]{0:T(1024)S(1)} %bitcast.138, bf16[2048,256]{1,0:T(8,128)(2,1)S(1)} %bitcast.125), kind=kCustom, calls=%fused_computation.57 | custom fusion | flops 1048576 | bytes 2097152 | tf_op jit(solution)/shard_map/scatter-add | solution.py:26
  169.8 1.0 copy-done.3
  170.8 150.9 %all-reduce.5.cloned.1.call-done = f32[8,8,32,32]{3,2,1,0:T(8,128)} async-done(((f32[8,8,32,32]{3,2,1,0:T(8,128)}), f32[8,8,32,32]{3,2,1,0:T(8,128)}) %all-reduce.5.cloned.1.call-update) | async-done | bytes 262160 | tf_op jit(solution)/shard_map/psum | solution.py:152
  321.6 51.3 %all-reduce.3.cloned.1.call-done = f32[1024,256]{1,0:T(8,128)} async-done(((f32[1024,256]{1,0:T(8,128)}), f32[1024,256]{1,0:T(8,128)}) %all-reduce.3.cloned.1.call-update) | async-done | bytes 1048592 | tf_op jit(solution)/shard_map/psum | solution.py:151
  372.9 2.3 copy.51
  375.2 1.0 copy.52
  (91 shorter events, 3.1 us)
Async XLA Ops:
  8.6 20.7 %all-to-all-start = ((s32[1,64,32]{2,0,1:T(1,128)}), s32[1,64,32]{2,0,1:T(1,128)S(1)}, u32[]{:S(2)}, u32[]{:S(2)}) async-start(s32[1,64,32]{2,0,1:T(1,128)} %copy.20), calls=%async_computation | async-start | bytes 65536 | tf_op jit(solution)/shard_map/all_to_all | solution.py:48
  29.2 1.3 copy-start.6
  47.0 6.5 %copy-start.8 = (s32[1024]{0:T(1024)S(1)}, s32[1024]{0:T(1024)}, u32[]{:S(2)}) copy-start(s32[1024]{0:T(1024)} %param.14) | copy-start | bytes 12292
  47.0 6.5 %copy-start.9 = (s32[1024]{0:T(1024)S(1)}, s32[1024]{0:T(1024)}, u32[]{:S(2)}) copy-start(s32[1024]{0:T(1024)} %param.15) | copy-start | bytes 12292
  47.0 6.6 %copy-start.10 = (s32[1024]{0:T(1024)S(1)}, s32[1024]{0:T(1024)}, u32[]{:S(2)}) copy-start(s32[1024]{0:T(1024)} %param.16) | copy-start | bytes 12292
  47.0 35.3 %all-to-all-start.1 = ((bf16[64,1,32,256]{3,2,1,0:T(8,128)(2,1)}), bf16[64,1,32,256]{3,2,1,0:T(8,128)(2,1)}, u32[]{:S(2)}, u32[]{:S(2)}) async-start(bf16[64,1,32,256]{3,2,1,0:T(8,128)(2,1)} %bitcast.1), calls=%async_computation.1 | async-start | bytes 2097152 | tf_op jit(solution)/shard_map/all_to_all | solution.py:52
  86.4 2.6 copy-start.5
  86.6 2.8 copy-start
  90.4 1.7 copy-start.1
  96.1 2.6 copy-start.5
  96.4 2.8 copy-start
  100.1 1.7 copy-start.1
  105.8 2.6 copy-start.5
  106.1 2.8 copy-start
  109.8 1.7 copy-start.1
  115.6 2.6 copy-start.5
  115.8 2.8 copy-start
  119.6 1.7 copy-start.1
  121.2 7.0 %copy-start.7 = (s32[1,64,32]{2,0,1:T(1,128)S(1)}, s32[1,64,32]{2,0,1:T(1,128)}, u32[]{:S(2)}) copy-start(s32[1,64,32]{2,0,1:T(1,128)} %copy-done.6) | copy-start | bytes 24580
  122.3 6.0 %copy-start.2 = (f32[8,8,32,32]{2,3,0,1:T(8,128)S(1)}, f32[8,8,32,32]{2,3,0,1:T(8,128)}, u32[]{:S(2)}) copy-start(f32[8,8,32,32]{2,3,0,1:T(8,128)} %get-tuple-element.138) | copy-start | bytes 786436
  122.3 35.4 %all-to-all-start.2 = ((bf16[1,64,32,256]{3,2,0,1:T(8,128)(2,1)}), bf16[1,64,32,256]{3,2,0,1:T(8,128)(2,1)S(1)}, u32[]{:S(2)}, u32[]{:S(2)}) async-start(bf16[1,64,32,256]{3,2,0,1:T(8,128)(2,1)} %bitcast.124), calls=%async_computation.2 | async-start | bytes 2097152 | tf_op jit(solution)/shard_map/all_to_all | solution.py:145
  128.2 1.6 copy-start.11
  128.2 193.4 %all-reduce.5.cloned.1.call-start = ((), (), s32[]{:S(2)}) async-start(), calls=%async_computation.4 | async-start | bytes 2097152 | tf_op jit(solution)/shard_map/psum | solution.py:152
  129.8 243.2 %all-reduce.3.cloned.1.call-start = ((), (), s32[]{:S(2)}) async-start(), calls=%async_computation.3 | async-start | bytes 2097152 | tf_op jit(solution)/shard_map/psum | solution.py:151
  169.8 1.0 copy-start.3
  321.6 53.6 %copy-start.4 = (f32[8,8,32,32]{3,2,1,0:T(8,128)S(1)}, f32[8,8,32,32]{3,2,1,0:T(8,128)}, u32[]{:S(2)}) copy-start(f32[8,8,32,32]{3,2,1,0:T(8,128)} %all-reduce.5.cloned.1.call-done) | copy-start | bytes 786436
Sparse Core Ops, SparseCore 0:
  132.4 189.1 all-reduce.4
  324.6 48.3 all-reduce.2
where the time goes:
time: 384 us; the launch traced here: 383 us
  waiting for transfers between devices  263 us (68%)
  matrix products  53.8 us (14%)
  starting transfers between devices  24.5 us (6%)
  other arithmetic  16.5 us (4%)
  between operations  14.2 us (4%)
  local copies, waits for them, and re-layouts  9.81 us (3%)
    psum x1, waiting for transfers between devices, local(): relation_grad = lax.psum(relation_acc, 'ent')  151 us
    psum x1, waiting for transfers between devices, local(): entity_grad = lax.psum(entity_acc, 'rel')  51.3 us
    all_to_all x1, waiting for transfers between devices, local(): lax.all_to_all(slot_grads.astype(jnp.bfloat16), 'ent', split_axis=1, conc...  27.4 us
    all_to_all x1, waiting for transfers between devices, local(): lax.all_to_all(wanted, 'ent', split_axis=0, concat_axis=1, tiled=True)  25.4 us
    dot_general x9, matrix products, pick_block(): jnp.dot(one_hot, source_table, preferred_element_type=jnp.float32)  17.8 us
    all_to_all x1, starting transfers between devices, local(): lax.all_to_all(request_rows, 'ent', split_axis=1, concat_axis=0, tiled=True)  12.1 us
    scatter-add x1, other arithmetic, owner_add(): return start_value.at[indices].add(gradients)  12 us
    all_to_all x1, waiting for transfers between devices, local(): lax.all_to_all(request_rows, 'ent', split_axis=1, concat_axis=0, tiled=True)  8.54 us
  transfers between devices with their start and end apart: 5, of which 5 were waited for; matrix products, arithmetic and copies ran while one was open for 5% of the time, Pallas kernels for 0%

commit v1 on v0

--- a/solution.py
+++ b/solution.py
@@ -148,7 +148,10 @@
     entity_acc = entity_acc + owner_add(
         owner_lists.reshape(-1), returned.reshape(-1, feature_width), entity_count
     )
-    entity_grad = lax.psum(entity_acc, "rel")
+    size, entity_grad = (lax.axis_size("rel"), entity_acc)
+    for reach in [1 << k for k in range(size.bit_length() - 1)]:
+        pairs = [(i, i ^ reach) for i in range(size)]
+        entity_grad = entity_grad + lax.ppermute(entity_grad, "rel", pairs)
     relation_grad = lax.psum(relation_acc, "ent")
     return (entity_grad, relation_grad)
 

time: 384 us -> 392 us (1.021)
  starting transfers between devices: 24.5 us -> 29.2 us
    psum x1 -> x0, waiting for transfers between devices: 51.3 us -> none  [local(): entity_grad = lax.psum(entity_acc, 'rel')]
    ppermute x0 -> x2, waiting for transfers between devices: none -> 42.7 us  [local(): entity_grad = entity_grad + lax.ppermute(entity_grad, 'rel', pairs)]
    psum x1, waiting for transfers between devices: 151 us -> 162 us  [local(): relation_grad = lax.psum(relation_acc, 'ent')]
    ppermute x0 -> x2, starting transfers between devices: none -> 4.68 us  [local(): entity_grad = entity_grad + lax.ppermute(entity_grad, 'rel', pairs)]
  transfers between devices with their start and end apart: 5 -> 6, of which waited for: 5 -> 6; matrix products, arithmetic and copies ran while one was open for 5% -> 2% of each run, Pallas kernels for 0% -> 0%
where the time goes in v1:
time: 392 us; the launch traced here: 390 us
  waiting for transfers between devices  266 us (68%)
  matrix products  53.8 us (14%)
  starting transfers between devices  29.2 us (7%)
  other arithmetic  18.2 us (5%)
  between operations  14.2 us (4%)
  local copies, waits for them, and re-layouts  7.81 us (2%)
    psum x1, waiting for transfers between devices, local(): relation_grad = lax.psum(relation_acc, 'ent')  162 us
    ppermute x2, waiting for transfers between devices, local(): entity_grad = entity_grad + lax.ppermute(entity_grad, 'rel', pairs)  42.7 us
    all_to_all x1, waiting for transfers between devices, local(): lax.all_to_all(slot_grads.astype(jnp.bfloat16), 'ent', split_axis=1, conc...  27.9 us
    all_to_all x1, waiting for transfers between devices, local(): lax.all_to_all(wanted, 'ent', split_axis=0, concat_axis=1, tiled=True)  25.4 us
    dot_general x9, matrix products, pick_block(): jnp.dot(one_hot, source_table, preferred_element_type=jnp.float32)  17.8 us
    scatter-add x1, other arithmetic, owner_add(): return start_value.at[indices].add(gradients)  12.4 us
    all_to_all x1, starting transfers between devices, local(): lax.all_to_all(request_rows, 'ent', split_axis=1, concat_axis=0, tiled=True)  12.1 us
    all_to_all x1, waiting for transfers between devices, local(): lax.all_to_all(request_rows, 'ent', split_axis=1, concat_axis=0, tiled=True)  8.54 us
  transfers between devices with their start and end apart: 6, of which 6 were waited for; matrix products, arithmetic and copies ran while one was open for 2% of the time, Pallas kernels for 0%

profile of v1, /device:TPU:8, one launch (start us, length us, event | category | flops | bytes accessed | tf_op | source)
XLA Modules:
  0.0 390.3 jit_solution(5676655966950386531)
XLA Ops:
  7.2 1.4 copy.20
  8.6 12.1 %all-to-all-start = ((s32[1,64,32]{2,0,1:T(1,128)}), s32[1,64,32]{2,0,1:T(1,128)S(1)}, u32[]{:S(2)}, u32[]{:S(2)}) async-start(s32[1,64,32]{2,0,1:T(1,128)} %copy.20), calls=%async_computation | async-start | bytes 65536 | tf_op jit(solution)/shard_map/all_to_all | solution.py:48
  20.7 8.5 %all-to-all-done = s32[1,64,32]{2,0,1:T(1,128)S(1)} async-done(((s32[1,64,32]{2,0,1:T(1,128)}), s32[1,64,32]{2,0,1:T(1,128)S(1)}, u32[]{:S(2)}, u32[]{:S(2)}) %all-to-all-start) | async-done | bytes 8224 | tf_op jit(solution)/shard_map/all_to_all | solution.py:48
  29.2 0.5 broadcast.122
  29.8 0.7 reduce.5
  30.6 16.5 %while.32 = (s32[]{:T(128)}, bf16[8,256,256]{2,1,0:T(8,128)(2,1)}, s32[8,256]{1,0:T(8,128)S(1)}, bf16[1024,256]{1,0:T(8,128)(2,1)}, s32[]{:T(128)}) while((s32[]{:T(128)}, bf16[8,256,256]{2,1,0:T(8,128)(2,1)}, s32[8,256]{1,0:T(8,128)S(1)}, bf16[1024,256]{1,0:T(8,128)(2,1)}, s32[]{:T(128)}) %tuple.56), condition=%wide.region_1.2_spmd.clone, body=%wide.region_0.1_spmd.clone.sunk | while | flops 134545408 | bytes 658509 | solution.py:20
  30.6 2.1 fusion.90
  32.6 2.0 fusion.90
  34.7 2.0 fusion.90
  36.8 2.1 fusion.90
  38.8 2.1 fusion.90
  40.9 2.0 fusion.90
  42.9 2.0 fusion.90
  45.0 2.1 fusion.90
  47.0 6.5 %all-to-all-start.1 = ((bf16[64,1,32,256]{3,2,1,0:T(8,128)(2,1)}), bf16[64,1,32,256]{3,2,1,0:T(8,128)(2,1)}, u32[]{:S(2)}, u32[]{:S(2)}) async-start(bf16[64,1,32,256]{3,2,1,0:T(8,128)(2,1)} %bitcast.1), calls=%async_computation.1 | async-start | bytes 2097152 | tf_op jit(solution)/shard_map/all_to_all | solution.py:52
  53.6 1.9 copy.21
  55.5 1.4 convolution_convert_fusion.2
  56.9 25.4 %all-to-all-done.1 = bf16[64,1,32,256]{3,2,1,0:T(8,128)(2,1)} async-done(((bf16[64,1,32,256]{3,2,1,0:T(8,128)(2,1)}), bf16[64,1,32,256]{3,2,1,0:T(8,128)(2,1)}, u32[]{:S(2)}, u32[]{:S(2)}) %all-to-all-start.1) | async-done | bytes 1048608 | tf_op jit(solution)/shard_map/all_to_all | solution.py:52
  82.3 38.9 %while.33 = (s32[]{:T(128)}, f32[2048,256]{1,0:T(8,128)S(1)}, f32[1024,256]{1,0:T(8,128)S(1)}, f32[256,256]{1,0:T(8,128)S(1)}, f32[8,8,32,32]{2,3,0,1:T(8,128)},...) while((s32[]{:T(128)}, f32[2048,256]{1,0:T(8,128)S(1)}, ...), condition=%wide.region_6.7_spmd.clone, body=%wide.region_2.6_spmd.clone.sunk | while | flops 1016077568 | bytes 14733582 | solution.py:137
  82.3 0.7 compare_convert_fusion.2
  83.0 1.5 convolution_convert_fusion.4
  84.5 1.5 fusion.110
  86.6 2.1 fusion.111
  89.0 0.4 fusion.114
  89.4 0.9 fusion.115
  90.4 0.6 convolution_add_fusion.9
  90.9 1.1 convolution_add_fusion.8
  92.0 0.7 compare_convert_fusion.2
  92.8 1.5 convolution_convert_fusion.4
  94.3 1.5 fusion.110
  96.4 2.1 fusion.111
  98.7 0.4 fusion.114
  99.1 0.9 fusion.115
  100.1 0.6 convolution_add_fusion.9
  100.7 1.1 convolution_add_fusion.8
  101.8 0.7 compare_convert_fusion.2
  102.5 1.5 convolution_convert_fusion.4
  104.0 1.5 fusion.110
  106.1 2.1 fusion.111
  108.4 0.4 fusion.114
  108.9 0.9 fusion.115
  109.8 0.6 convolution_add_fusion.9
  110.4 1.1 convolution_add_fusion.8
  111.5 0.7 compare_convert_fusion.2
  112.2 1.5 convolution_convert_fusion.4
  113.7 1.5 fusion.110
  115.8 2.1 fusion.111
  118.2 0.4 fusion.114
  118.6 0.9 fusion.115
  119.6 0.6 convolution_add_fusion.9
  120.2 1.1 convolution_add_fusion.8
  121.3 1.1 convert_element_type.106
  122.3 5.9 %all-to-all-start.2 = ((bf16[1,64,32,256]{3,2,0,1:T(8,128)(2,1)}), bf16[1,64,32,256]{3,2,0,1:T(8,128)(2,1)}, u32[]{:S(2)}, u32[]{:S(2)}) async-start(bf16[1,64,32,256]{3,2,0,1:T(8,128)(2,1)} %bitcast.124), calls=%async_computation.2 | async-start | bytes 2097152 | tf_op jit(solution)/shard_map/all_to_all | solution.py:145
  128.4 0.6 convolution_add_fusion.4
  129.0 27.9 %all-to-all-done.2 = bf16[1,64,32,256]{3,2,0,1:T(8,128)(2,1)} async-done(((bf16[1,64,32,256]{3,2,0,1:T(8,128)(2,1)}), bf16[1,64,32,256]{3,2,0,1:T(8,128)(2,1)}, u32[]{:S(2)}, u32[]{:S(2)}) %all-to-all-start.2) | async-done | bytes 1048608 | tf_op jit(solution)/shard_map/all_to_all | solution.py:145
  156.9 12.4 %scatter_custom_fusion = f32[1024,256]{1,0:T(8,128)S(1)} fusion(f32[1024,256]{1,0:T(8,128)S(1)} %convolution_add_fusion.4, s32[2048]{0:T(1024)S(1)} %bitcast.137, bf16[2048,256]{1,0:T(8,128)(2,1)} %bitcast.25), kind=kCustom, calls=%fused_computation.57 | custom fusion | flops 1048576 | bytes 2097152 | tf_op jit(solution)/shard_map/scatter-add | solution.py:26
  169.4 1.6 collective-permute-start
  171.0 22.4 %collective-permute-done = f32[1024,256]{1,0:T(8,128)S(1)} collective-permute-done((f32[1024,256]{1,0:T(8,128)S(1)}, f32[1024,256]{1,0:T(8,128)S(1)}, u32[]{:S(2)}, u32[]{:S(2)}) %collective-permute-start) | collective-permute-done | bytes 1048608 | tf_op jit(solution)/shard_map/ppermute | solution.py:154
  193.5 3.1 collective-permute-start.1
  196.6 1.3 copy.22
  198.0 20.2 %collective-permute-done.1 = f32[1024,256]{1,0:T(8,128)S(1)} collective-permute-done((f32[1024,256]{1,0:T(8,128)S(1)}, f32[1024,256]{1,0:T(8,128)S(1)}, u32[]{:S(2)}, u32[]{:S(2)}) %collective-permute-start.1) | collective-permute-done | bytes 1048608 | tf_op jit(solution)/shard_map/ppermute | solution.py:154
  218.2 1.1 add.66
  219.3 161.9 %all-reduce.2.cloned.1.call-done = f32[8,8,32,32]{3,2,1,0:T(8,128)} async-done(((f32[8,8,32,32]{3,2,1,0:T(8,128)}), f32[8,8,32,32]{3,2,1,0:T(8,128)}) %all-reduce.2.cloned.1.call-update) | async-done | bytes 262160 | tf_op jit(solution)/shard_map/psum | solution.py:155
  381.2 2.3 copy.50
  (89 shorter events, 3.7 us)
Async XLA Ops:
  8.6 20.7 %all-to-all-start = ((s32[1,64,32]{2,0,1:T(1,128)}), s32[1,64,32]{2,0,1:T(1,128)S(1)}, u32[]{:S(2)}, u32[]{:S(2)}) async-start(s32[1,64,32]{2,0,1:T(1,128)} %copy.20), calls=%async_computation | async-start | bytes 65536 | tf_op jit(solution)/shard_map/all_to_all | solution.py:48
  29.2 1.3 copy-start.4
  47.0 6.5 %copy-start.6 = (s32[1024]{0:T(1024)S(1)}, s32[1024]{0:T(1024)}, u32[]{:S(2)}) copy-start(s32[1024]{0:T(1024)} %param.14) | copy-start | bytes 12292
  47.0 6.5 %copy-start.7 = (s32[1024]{0:T(1024)S(1)}, s32[1024]{0:T(1024)}, u32[]{:S(2)}) copy-start(s32[1024]{0:T(1024)} %param.15) | copy-start | bytes 12292
  47.0 6.6 %copy-start.8 = (s32[1024]{0:T(1024)S(1)}, s32[1024]{0:T(1024)}, u32[]{:S(2)}) copy-start(s32[1024]{0:T(1024)} %param.16) | copy-start | bytes 12292
  47.0 35.3 %all-to-all-start.1 = ((bf16[64,1,32,256]{3,2,1,0:T(8,128)(2,1)}), bf16[64,1,32,256]{3,2,1,0:T(8,128)(2,1)}, u32[]{:S(2)}, u32[]{:S(2)}) async-start(bf16[64,1,32,256]{3,2,1,0:T(8,128)(2,1)} %bitcast.1), calls=%async_computation.1 | async-start | bytes 2097152 | tf_op jit(solution)/shard_map/all_to_all | solution.py:52
  86.4 2.6 copy-start.3
  86.6 2.8 copy-start
  90.4 1.7 copy-start.1
  96.1 2.6 copy-start.3
  96.4 2.8 copy-start
  100.1 1.7 copy-start.1
  105.8 2.6 copy-start.3
  106.1 2.8 copy-start
  109.8 1.7 copy-start.1
  115.6 2.6 copy-start.3
  115.8 2.8 copy-start
  119.6 1.7 copy-start.1
  121.2 7.1 %copy-start.5 = (s32[1,64,32]{2,0,1:T(1,128)S(1)}, s32[1,64,32]{2,0,1:T(1,128)}, u32[]{:S(2)}) copy-start(s32[1,64,32]{2,0,1:T(1,128)} %copy-done.4) | copy-start | bytes 24580
  121.2 7.2 %copy-start.9 = (s32[256]{0:T(256)S(1)}, s32[256]{0:T(256)}, u32[]{:S(2)}) copy-start(s32[256]{0:T(256)} %param.18) | copy-start | bytes 3076
  122.3 34.6 %all-to-all-start.2 = ((bf16[1,64,32,256]{3,2,0,1:T(8,128)(2,1)}), bf16[1,64,32,256]{3,2,0,1:T(8,128)(2,1)}, u32[]{:S(2)}, u32[]{:S(2)}) async-start(bf16[1,64,32,256]{3,2,0,1:T(8,128)(2,1)} %bitcast.124), calls=%async_computation.2 | async-start | bytes 2097152 | tf_op jit(solution)/shard_map/all_to_all | solution.py:145
  128.3 252.9 %all-reduce.2.cloned.1.call-start = ((), (), s32[]{:S(2)}) async-start(), calls=%async_computation.3 | async-start | bytes 2097152 | tf_op jit(solution)/shard_map/psum | solution.py:155
  169.4 27.3 %copy-start.2 = (f32[8,8,32,32]{2,3,0,1:T(8,128)S(1)}, f32[8,8,32,32]{2,3,0,1:T(8,128)}, u32[]{:S(2)}) copy-start(f32[8,8,32,32]{2,3,0,1:T(8,128)} %get-tuple-element.138) | copy-start | bytes 786436
  169.4 24.0 %collective-permute-start = (f32[1024,256]{1,0:T(8,128)S(1)}, f32[1024,256]{1,0:T(8,128)S(1)}, u32[]{:S(2)}, u32[]{:S(2)}) collective-permute-start(f32[1024,256]{1,0:T(8,128)S(1)} %scatter_custom_fusion), channel_id=1, source_target_pairs={{0,1},{1,0},{2,3},{3,2},{4,5},{5,4},{6,7},{7,6},{8,9},{9,8},{10,11... | collective-permute-start | bytes 3145736 | tf_op jit(solution)/shard_map/ppermute | solution.py:154
  193.5 24.7 %collective-permute-start.1 = (f32[1024,256]{1,0:T(8,128)S(1)}, f32[1024,256]{1,0:T(8,128)S(1)}, u32[]{:S(2)}, u32[]{:S(2)}) collective-permute-start(f32[1024,256]{1,0:T(8,128)S(1)} %add.65), channel_id=1, source_target_pairs={{0,2},{1,3},{2,0},{3,1},{4,6},{5,7},{6,4},{7,5},{8,10},{9,11},{10,... | collective-permute-start | bytes 3145736 | tf_op jit(solution)/shard_map/ppermute | solution.py:154
Sparse Core Ops, SparseCore 0:
  198.1 183.0 all-reduce.1
